TPU v7x, 32 devices: a whole 2x2x4 slice. The times are simulated.
32 devices in a mesh: row: 16 (over z, y, core), col: 2 (over x).
Axes of the slice: x: 2, y: 2, z: 4, core: 2. Of those that a mesh axis runs over, the one named last changes fastest.
Arguments:
- start_block: float32 [4096, 256], P(('row', 'col')), may hold values from -6 to 6
- tiles: bfloat16 [16, 2, 14, 128, 128], P('row', 'col'), may hold values from -0.125 to 0.125
- tile_rows: int32 [16, 2, 14], P('row', 'col'), may hold values from -1 to 31, as said below
- tile_cols: int32 [16, 2, 14], P('row', 'col'), may hold values from -1 to 31, as said below
- bounds: float32 [3], replicated, may hold values from -2.6 to 2.6, as said below
Outputs:
- filtered: float32 [4096, 256], P(('row', 'col'))
Inputs may be any that keep to these rules, and one draw needn't show every extreme that they name: Vector rows form blocks of 128 rows, one block a device, in row+col order. On the device at grid row r and grid column c, a live slot names a block row held by one of the devices (r, any column) and a block column held by one of the devices (any row, c). Live slots come first; each device has 1 to 14 live slots, and one device has exactly 14 in every draw. No block position is named twice, and the mirror of a named position is never named unless it lies on the diagonal. tile_rows and tile_cols are -1 together. `tile_cols`: same slots as tile_rows. bounds[0] < bounds[1] < bounds[2].
All inputs are finite; a program needn't handle non-finite values.
Results may differ from a plain program's by a relative error of at most 0.0042.
Values may be sent and summed in bfloat16 or wider, within the bound.
A program may use at most 64 MiB of HBM per device.

v0:
```python
import jax
import jax.numpy as jnp
from jax import lax
from jax.sharding import PartitionSpec as P

DEGREE = 4


def local(start_block, tiles, tile_rows, tile_cols, bounds):
    rows_dev, vec_width = start_block.shape
    tile_size = tiles.shape[-1]
    blocks = rows_dev // tile_size
    row_count = lax.axis_size("row")
    col_count = lax.axis_size("col")
    near_count = col_count * blocks
    far_count = row_count * blocks
    row_index = lax.axis_index("row")
    col_index = lax.axis_index("col")
    slots = tiles.shape[2]
    tile_mats = tiles.reshape(slots, tile_size, tile_size)
    glob_rows = tile_rows.reshape(slots)
    glob_cols = tile_cols.reshape(slots)
    is_live = glob_rows >= 0
    local_rows = jnp.where(is_live, glob_rows - row_index * near_count, -1)
    local_cols = jnp.where(
        is_live, glob_cols // blocks // col_count * blocks + glob_cols % blocks, -1
    )
    slot_place = jnp.where(is_live, local_rows * far_count + local_cols, near_count * far_count)
    owned = jnp.zeros((near_count * far_count, tile_size, tile_size), jnp.bfloat16)
    owned = owned.at[slot_place].add(tile_mats, mode="drop")
    owned = owned.reshape(col_count, blocks, row_count, blocks, tile_size, tile_size)
    received = lax.all_to_all(
        lax.all_to_all(owned, "row", split_axis=2, concat_axis=2, tiled=True),
        "col",
        split_axis=0,
        concat_axis=0,
        tiled=True,
    )
    mirror = jnp.transpose(received, (0, 3, 2, 1, 5, 4))
    grid_shape = (col_count, blocks, row_count, blocks)
    col_grid = lax.broadcasted_iota(jnp.int32, grid_shape, 0)
    first_sub = lax.broadcasted_iota(jnp.int32, grid_shape, 1)
    row_grid = lax.broadcasted_iota(jnp.int32, grid_shape, 2)
    second_sub = lax.broadcasted_iota(jnp.int32, grid_shape, 3)
    on_diagonal = (col_grid == col_index) & (row_grid == row_index) & (first_sub == second_sub)
    zero_tile = jnp.zeros((), jnp.bfloat16)
    window = (jnp.where(on_diagonal[..., None, None], zero_tile, owned) + mirror).reshape(
        near_count, far_count, tile_size, tile_size
    )
    owned_here = lax.dynamic_index_in_dim(owned, col_index, 0, keepdims=False)
    owned_here = lax.dynamic_index_in_dim(owned_here, row_index, 1, keepdims=False)
    block_ids = jnp.arange(blocks)
    diagonal_tiles = owned_here[block_ids, block_ids]

    def apply_matrix(vectors):
        low_vectors = vectors.astype(jnp.bfloat16)
        far_vectors = lax.all_gather(low_vectors, "row", axis=0, tiled=True).reshape(
            far_count, tile_size, vec_width
        )
        near_partial = jnp.einsum(
            "apxy,pyk->axk", window, far_vectors, preferred_element_type=jnp.float32
        )
        own_vectors = lax.dynamic_slice_in_dim(far_vectors, row_index * blocks, blocks, 0)
        diagonal_part = jnp.einsum(
            "uxy,uyk->uxk", diagonal_tiles, own_vectors, preferred_element_type=jnp.float32
        )
        current_rows = lax.dynamic_slice_in_dim(near_partial, col_index * blocks, blocks, 0)
        near_partial = lax.dynamic_update_slice_in_dim(
            near_partial, current_rows + diagonal_part, col_index * blocks, 0
        )
        combined = lax.psum_scatter(
            near_partial.reshape(near_count * tile_size, vec_width),
            "col",
            scatter_dimension=0,
            tiled=True,
        )
        return combined

    half_width = (bounds[2] - bounds[1]) * 0.5
    center = (bounds[2] + bounds[1]) * 0.5
    sigma_one = half_width / (bounds[0] - center)
    previous = start_block
    current = (apply_matrix(start_block) - center * start_block) * (sigma_one / half_width)
    sigma = sigma_one
    for turn_index in range(DEGREE - 1):
        sigma_next = 1.0 / (2.0 / sigma_one - sigma)
        product = apply_matrix(current)
        following = (product - center * current) * (
            2.0 * sigma_next / half_width
        ) - sigma * sigma_next * previous
        previous = current
        current = following
        sigma = sigma_next
    return current


def solution(mesh):
    placed = (
        P(("row", "col"), None),
        P("row", "col", None, None, None),
        P("row", "col", None),
        P("row", "col", None),
        P(),
    )
    return jax.shard_map(
        local, mesh=mesh, in_specs=placed, out_specs=P(("row", "col"), None), check_vma=False
    )
```

profile of v0, /device:TPU:0, one launch (start us, length us, event | category | flops | bytes accessed | tf_op | source)
XLA Modules:
  0.0 251.6 jit_solution(16781734857981256183)
XLA Ops:
  8.2 2.1 scatter_fusion
  10.3 1.3 copy.9
  11.6 7.5 %all-to-all-start = ((bf16[2,1,16,1,128,128]{4,5,0,1,3,2:T(8,128)(2,1)}), bf16[2,1,16,1,128,128]{4,5,0,1,3,2:T(8,128)(2,1)S(1)}, u32[]{:S(2)}, u32[]{:S(2)}) async-start(bf16[2,1,16,1,128,128]{4,5,0,1,3,2:T(8,128)(2,1)} %copy.9), calls=%async_computation | async-start | bytes 2097152 | tf_op jit(solution)/shard_map/all_to_all | solution.py:33
  19.9 23.3 %all-to-all-done = bf16[2,1,16,1,128,128]{4,5,0,1,3,2:T(8,128)(2,1)S(1)} async-done(((bf16[2,1,16,1,128,128]{4,5,0,1,3,2:T(8,128)(2,1)}), bf16[2,1,16,1,128,128]{4,5,0,1,3,2:T(8,128)(2,1)S(1)}, u32[]{:S(2)}, u32[]{:S(2)}) %all-to-all-start) | async-done | bytes 1048608 | tf_op jit(solution)/shard_map/all_to_all | solution.py:33
  43.2 1.1 copy.10
  44.3 3.6 %all-to-all-start.1 = ((bf16[2,1,16,1,128,128]{4,5,2,1,3,0:T(8,128)(2,1)}), bf16[2,1,16,1,128,128]{4,5,2,1,3,0:T(8,128)(2,1)S(1)}, u32[]{:S(2)}, u32[]{:S(2)}) async-start(bf16[2,1,16,1,128,128]{4,5,2,1,3,0:T(8,128)(2,1)} %copy.10), calls=%async_computation.1 | async-start | bytes 2097152 | tf_op jit(solution)/shard_map/all_to_all | solution.py:32
  48.0 14.3 %all-to-all-done.1 = bf16[2,1,16,1,128,128]{4,5,2,1,3,0:T(8,128)(2,1)S(1)} async-done(((bf16[2,1,16,1,128,128]{4,5,2,1,3,0:T(8,128)(2,1)}), bf16[2,1,16,1,128,128]{4,5,2,1,3,0:T(8,128)(2,1)S(1)}, u32[]{:S(2)}, u32[]{:S(2)}) %all-to-all-start.1) | async-done | bytes 1048608 | tf_op jit(solution)/shard_map/all_to_all | solution.py:32
  62.5 3.5 %all-gather.5.cloned.1.call-done = bf16[2048,256]{1,0:T(8,128)(2,1)} async-done(((bf16[128,256]{1,0:T(8,128)(2,1)}), bf16[2048,256]{1,0:T(8,128)(2,1)}) %all-gather.5.cloned.1.call-update) | async-done | bytes 1048592 | tf_op jit(solution)/shard_map/all_gather | solution.py:57
  66.0 1.7 convolution_bitcast_fusion.3
  67.6 1.0 fusion.1
  73.3 6.9 %reduce-scatter.5.cloned.1.call-done = f32[128,256]{1,0:T(8,128)} async-done(((f32[256,256]{1,0:T(8,128)}), f32[128,256]{1,0:T(8,128)}) %reduce-scatter.5.cloned.1.call-update) | async-done | bytes 131088 | tf_op jit(solution)/shard_map/reduce_scatter | solution.py:71
  80.2 1.6 fusion.37
  81.8 38.4 %all-gather.7.cloned.1.call-done = bf16[2048,256]{1,0:T(8,128)(2,1)} async-done(((bf16[128,256]{1,0:T(8,128)(2,1)}), bf16[2048,256]{1,0:T(8,128)(2,1)}) %all-gather.7.cloned.1.call-update) | async-done | bytes 1048592 | tf_op jit(solution)/shard_map/all_gather | solution.py:57
  120.3 1.7 convolution_bitcast_fusion.2
  123.9 10.7 %reduce-scatter.7.cloned.1.call-done = f32[128,256]{1,0:T(8,128)} async-done(((f32[256,256]{1,0:T(8,128)}), f32[128,256]{1,0:T(8,128)}) %reduce-scatter.7.cloned.1.call-update) | async-done | bytes 131088 | tf_op jit(solution)/shard_map/reduce_scatter | solution.py:71
  134.6 1.6 fusion.36
  136.2 38.3 %all-gather.9.cloned.1.call-done = bf16[2048,256]{1,0:T(8,128)(2,1)} async-done(((bf16[128,256]{1,0:T(8,128)(2,1)}), bf16[2048,256]{1,0:T(8,128)(2,1)}) %all-gather.9.cloned.1.call-update) | async-done | bytes 1048592 | tf_op jit(solution)/shard_map/all_gather | solution.py:57
  174.5 1.7 convolution_bitcast_fusion.1
  178.0 10.8 %reduce-scatter.9.cloned.1.call-done = f32[128,256]{1,0:T(8,128)} async-done(((f32[256,256]{1,0:T(8,128)}), f32[128,256]{1,0:T(8,128)}) %reduce-scatter.9.cloned.1.call-update) | async-done | bytes 131088 | tf_op jit(solution)/shard_map/reduce_scatter | solution.py:71
  188.8 1.6 fusion.24
  190.4 38.4 %all-gather.11.cloned.1.call-done = bf16[2048,256]{1,0:T(8,128)(2,1)} async-done(((bf16[128,256]{1,0:T(8,128)(2,1)}), bf16[2048,256]{1,0:T(8,128)(2,1)}) %all-gather.11.cloned.1.call-update) | async-done | bytes 1048592 | tf_op jit(solution)/shard_map/all_gather | solution.py:57
  228.8 1.7 convolution_bitcast_fusion
  232.3 10.8 %reduce-scatter.11.cloned.1.call-done = f32[128,256]{1,0:T(8,128)} async-done(((f32[256,256]{1,0:T(8,128)}), f32[128,256]{1,0:T(8,128)}) %reduce-scatter.11.cloned.1.call-update) | async-done | bytes 131088 | tf_op jit(solution)/shard_map/reduce_scatter | solution.py:71
  243.1 1.6 multiply_subtract_fusion
  (47 shorter events, 9.5 us)
Async XLA Ops:
  6.5 0.7 copy-start.8
  6.5 0.7 copy-start.9
  7.2 1.0 copy-start.6
  11.6 7.6 %copy-start.4 = (f32[128,256]{1,0:T(8,128)S(1)}, f32[128,256]{1,0:T(8,128)}, u32[]{:S(2)}) copy-start(f32[128,256]{1,0:T(8,128)} %param.5) | copy-start | bytes 393220
  11.6 31.6 %all-to-all-start = ((bf16[2,1,16,1,128,128]{4,5,0,1,3,2:T(8,128)(2,1)}), bf16[2,1,16,1,128,128]{4,5,0,1,3,2:T(8,128)(2,1)S(1)}, u32[]{:S(2)}, u32[]{:S(2)}) async-start(bf16[2,1,16,1,128,128]{4,5,0,1,3,2:T(8,128)(2,1)} %copy.9), calls=%async_computation | async-start | bytes 2097152 | tf_op jit(solution)/shard_map/all_to_all | solution.py:33
  19.2 46.8 %all-gather.5.cloned.1.call-start = ((), (), s32[]{:S(2)}) async-start(), calls=%async_computation.6 | async-start | bytes 1114112 | tf_op jit(solution)/shard_map/all_gather | solution.py:57
  44.3 18.0 %all-to-all-start.1 = ((bf16[2,1,16,1,128,128]{4,5,2,1,3,0:T(8,128)(2,1)}), bf16[2,1,16,1,128,128]{4,5,2,1,3,0:T(8,128)(2,1)S(1)}, u32[]{:S(2)}, u32[]{:S(2)}) async-start(bf16[2,1,16,1,128,128]{4,5,2,1,3,0:T(8,128)(2,1)} %copy.10), calls=%async_computation.1 | async-start | bytes 2097152 | tf_op jit(solution)/shard_map/all_to_all | solution.py:32
  47.9 32.4 %reduce-scatter.5.cloned.1.call-start = ((), (), s32[]{:S(2)}) async-start(), calls=%async_computation.7 | async-start | bytes 393216 | tf_op jit(solution)/shard_map/reduce_scatter | solution.py:71
  68.6 0.7 copy-start.1
  68.6 0.8 copy-start.7
  69.3 50.9 %all-gather.7.cloned.1.call-start = ((), (), s32[]{:S(2)}) async-start(), calls=%async_computation.8 | async-start | bytes 1114112 | tf_op jit(solution)/shard_map/all_gather | solution.py:57
  81.8 52.8 %reduce-scatter.7.cloned.1.call-start = ((), (), s32[]{:S(2)}) async-start(), calls=%async_computation.9 | async-start | bytes 393216 | tf_op jit(solution)/shard_map/reduce_scatter | solution.py:71
  122.9 0.7 copy-start.2
  123.7 50.8 %all-gather.9.cloned.1.call-start = ((), (), s32[]{:S(2)}) async-start(), calls=%async_computation.10 | async-start | bytes 1114112 | tf_op jit(solution)/shard_map/all_gather | solution.py:57
  136.1 52.6 %reduce-scatter.9.cloned.1.call-start = ((), (), s32[]{:S(2)}) async-start(), calls=%async_computation.11 | async-start | bytes 393216 | tf_op jit(solution)/shard_map/reduce_scatter | solution.py:71
  177.1 0.7 copy-start.3
  177.9 51.0 %all-gather.11.cloned.1.call-start = ((), (), s32[]{:S(2)}) async-start(), calls=%async_computation.12 | async-start | bytes 1114112 | tf_op jit(solution)/shard_map/all_gather | solution.py:57
  190.3 52.8 %reduce-scatter.11.cloned.1.call-start = ((), (), s32[]{:S(2)}) async-start(), calls=%async_computation.13 | async-start | bytes 393216 | tf_op jit(solution)/shard_map/reduce_scatter | solution.py:71
  231.5 0.7 copy-start
  231.5 11.6 %copy-start.5 = (f32[128,256]{1,0:T(8,128)S(1)}, f32[128,256]{1,0:T(8,128)}, u32[]{:S(2)}) copy-start(f32[128,256]{1,0:T(8,128)} %reduce-scatter.9.cloned.1.call-done) | copy-start | bytes 393220
Sparse Core Ops, SparseCore 0:
  22.2 43.7 all-gather.4
  69.5 10.6 reduce-scatter.4
  82.4 37.8 all-gather.6
  123.8 10.7 reduce-scatter.6
  136.6 37.8 all-gather.8
  178.0 10.7 reduce-scatter.8
  190.9 37.8 all-gather.10
  232.3 10.7 reduce-scatter.10
where the time goes:
time: 252 us
  waiting for transfers between devices  195 us (77%)
  between operations  17.3 us (7%)
  starting transfers between devices  11.5 us (5%)
  matrix products  10.6 us (4%)
  other arithmetic  9.26 us (4%)
  local copies, waits for them, and re-layouts  7.5 us (3%)
    all_gather x4, waiting for transfers between devices, apply_matrix(): lax.all_gather(low_vectors, 'row', axis=0, tiled=True)  119 us
    reduce_scatter x4, waiting for transfers between devices, apply_matrix(): lax.psum_scatter(near_partial.reshape(near_count * tile_size, vec_width),...  39.2 us
    all_to_all x1, waiting for transfers between devices, local(): lax.all_to_all(owned, 'row', split_axis=2, concat_axis=2, tiled=True)  23.3 us
    all_to_all x1, waiting for transfers between devices, local(): lax.all_to_all(lax.all_to_all(owned, 'row', split_axis=2, concat_axis=2,...  14.3 us
    all_to_all x1, starting transfers between devices, local(): lax.all_to_all(owned, 'row', split_axis=2, concat_axis=2, tiled=True)  7.55 us
    dot_general x4, matrix products, apply_matrix(): jnp.einsum('apxy,pyk->axk', window, far_vectors, preferred_element_type=j...  6.63 us
    convert_element_type x4, other arithmetic, apply_matrix(): low_vectors = vectors.astype(jnp.bfloat16)  5.32 us
  transfers between devices with their start and end apart: 10, of which 10 were waited for; matrix products, arithmetic and copies ran while one was open for 1% of the time, Pallas kernels for 0%

commit v1 on v0

--- a/solution.py
+++ b/solution.py
@@ -30,7 +30,10 @@
     owned = owned.at[slot_place].add(tile_mats, mode="drop")
     owned = owned.reshape(col_count, blocks, row_count, blocks, tile_size, tile_size)
     received = lax.all_to_all(
-        lax.all_to_all(owned, "row", split_axis=2, concat_axis=2, tiled=True),
+        jnp.concatenate(
+            lax.all_to_all(jnp.stack(jnp.split(owned, lax.axis_size("row"), axis=2)), "row", 0, 0),
+            axis=2,
+        ),
         "col",
         split_axis=0,
         concat_axis=0,

time: 252 us -> 262 us (1.040)
  local copies, waits for them, and re-layouts: 7.5 us -> 16.9 us
    unnamed x20 -> x35, local copies, waits for them, and re-layouts: 4.23 us -> 13.7 us
where the time goes in v1:
time: 262 us; the launch traced here: 261 us
  waiting for transfers between devices  195 us (74%)
  between operations  17.3 us (7%)
  local copies, waits for them, and re-layouts  16.9 us (6%)
  starting transfers between devices  11.5 us (4%)
  matrix products  10.6 us (4%)
  other arithmetic  9.26 us (4%)
    all_gather x4, waiting for transfers between devices, apply_matrix(): lax.all_gather(low_vectors, 'row', axis=0, tiled=True)  118 us
    reduce_scatter x4, waiting for transfers between devices, apply_matrix(): lax.psum_scatter(near_partial.reshape(near_count * tile_size, vec_width),...  39.7 us
    all_to_all x1, waiting for transfers between devices, local(): lax.all_to_all(jnp.stack(jnp.split(owned, lax.axis_size('row'), axis=2)),...  23.3 us
    all_to_all x1, waiting for transfers between devices, local(): lax.all_to_all(jnp.concatenate(lax.all_to_all(jnp.stack(jnp.split(owned,...  14.3 us
    unnamed x35, local copies, waits for them, and re-layouts  13.7 us
    all_to_all x1, starting transfers between devices, local(): lax.all_to_all(jnp.stack(jnp.split(owned, lax.axis_size('row'), axis=2)),...  7.55 us
    dot_general x4, matrix products, apply_matrix(): jnp.einsum('apxy,pyk->axk', window, far_vectors, preferred_element_type=j...  6.63 us
    convert_element_type x4, other arithmetic, apply_matrix(): low_vectors = vectors.astype(jnp.bfloat16)  5.32 us
  transfers between devices with their start and end apart: 10, of which 10 were waited for; matrix products, arithmetic and copies ran while one was open for 1% of the time, Pallas kernels for 0%

profile of v1, /device:TPU:0, one launch (start us, length us, event | category | flops | bytes accessed | tf_op | source)
XLA Modules:
  0.0 260.8 jit_solution(9959051007246926803)
XLA Ops:
  8.2 2.1 scatter_fusion
  20.4 7.5 %all-to-all-start = ((bf16[16,2,1,1,1,128,128]{6,5,1,4,3,2,0:T(8,128)(2,1)}), bf16[16,2,1,1,1,128,128]{6,5,1,4,3,2,0:T(8,128)(2,1)S(1)}, u32[]{:S(2)}, u32[]{:S(2)}) async-start(bf16[16,2,1,1,1,128,128]{6,5,1,4,3,2,0:T(8,128)(2,1)} %fusion.12), calls=%async_computation | async-start | bytes 2097152 | tf_op jit(solution)/shard_map/all_to_all | solution.py:34
  28.7 23.3 %all-to-all-done = bf16[16,2,1,1,1,128,128]{6,5,1,4,3,2,0:T(8,128)(2,1)S(1)} async-done(((bf16[16,2,1,1,1,128,128]{6,5,1,4,3,2,0:T(8,128)(2,1)}), bf16[16,2,1,1,1,128,128]{6,5,1,4,3,2,0:T(8,128)(2,1)S(1)}, u32[]{:S(2)}, u32[]{:S(2)}) %all-to-all-start) | async-done | bytes 1048608 | tf_op jit(solution)/shard_map/all_to_all | solution.py:34
  52.0 1.1 copy.57
  53.1 3.6 %all-to-all-start.1 = ((bf16[2,1,16,1,128,128]{5,4,2,3,1,0:T(8,128)(2,1)}), bf16[2,1,16,1,128,128]{5,4,2,3,1,0:T(8,128)(2,1)S(1)}, u32[]{:S(2)}, u32[]{:S(2)}) async-start(bf16[2,1,16,1,128,128]{5,4,2,3,1,0:T(8,128)(2,1)} %copy.57), calls=%async_computation.1 | async-start | bytes 2097152 | tf_op jit(solution)/shard_map/all_to_all | solution.py:32
  56.8 14.3 %all-to-all-done.1 = bf16[2,1,16,1,128,128]{5,4,2,3,1,0:T(8,128)(2,1)S(1)} async-done(((bf16[2,1,16,1,128,128]{5,4,2,3,1,0:T(8,128)(2,1)}), bf16[2,1,16,1,128,128]{5,4,2,3,1,0:T(8,128)(2,1)S(1)}, u32[]{:S(2)}, u32[]{:S(2)}) %all-to-all-start.1) | async-done | bytes 1048608 | tf_op jit(solution)/shard_map/all_to_all | solution.py:32
  71.9 2.8 %all-gather.5.cloned.1.call-done = bf16[2048,256]{1,0:T(8,128)(2,1)} async-done(((bf16[128,256]{1,0:T(8,128)(2,1)}), bf16[2048,256]{1,0:T(8,128)(2,1)}) %all-gather.5.cloned.1.call-update) | async-done | bytes 1048592 | tf_op jit(solution)/shard_map/all_gather | solution.py:60
  74.7 1.7 convolution_bitcast_fusion.3
  76.4 1.0 fusion.1
  82.1 7.4 %reduce-scatter.5.cloned.1.call-done = f32[128,256]{1,0:T(8,128)} async-done(((f32[256,256]{1,0:T(8,128)}), f32[128,256]{1,0:T(8,128)}) %reduce-scatter.5.cloned.1.call-update) | async-done | bytes 131088 | tf_op jit(solution)/shard_map/reduce_scatter | solution.py:74
  89.5 1.6 fusion.53
  91.1 38.4 %all-gather.7.cloned.1.call-done = bf16[2048,256]{1,0:T(8,128)(2,1)} async-done(((bf16[128,256]{1,0:T(8,128)(2,1)}), bf16[2048,256]{1,0:T(8,128)(2,1)}) %all-gather.7.cloned.1.call-update) | async-done | bytes 1048592 | tf_op jit(solution)/shard_map/all_gather | solution.py:60
  129.5 1.7 convolution_bitcast_fusion.2
  131.2 1.0 fusion.3
  133.2 10.7 %reduce-scatter.7.cloned.1.call-done = f32[128,256]{1,0:T(8,128)} async-done(((f32[256,256]{1,0:T(8,128)}), f32[128,256]{1,0:T(8,128)}) %reduce-scatter.7.cloned.1.call-update) | async-done | bytes 131088 | tf_op jit(solution)/shard_map/reduce_scatter | solution.py:74
  143.8 1.6 fusion.52
  145.5 38.3 %all-gather.9.cloned.1.call-done = bf16[2048,256]{1,0:T(8,128)(2,1)} async-done(((bf16[128,256]{1,0:T(8,128)(2,1)}), bf16[2048,256]{1,0:T(8,128)(2,1)}) %all-gather.9.cloned.1.call-update) | async-done | bytes 1048592 | tf_op jit(solution)/shard_map/all_gather | solution.py:60
  183.7 1.7 convolution_bitcast_fusion.1
  187.3 10.8 %reduce-scatter.9.cloned.1.call-done = f32[128,256]{1,0:T(8,128)} async-done(((f32[256,256]{1,0:T(8,128)}), f32[128,256]{1,0:T(8,128)}) %reduce-scatter.9.cloned.1.call-update) | async-done | bytes 131088 | tf_op jit(solution)/shard_map/reduce_scatter | solution.py:74
  198.0 1.6 fusion.40
  199.7 38.4 %all-gather.11.cloned.1.call-done = bf16[2048,256]{1,0:T(8,128)(2,1)} async-done(((bf16[128,256]{1,0:T(8,128)(2,1)}), bf16[2048,256]{1,0:T(8,128)(2,1)}) %all-gather.11.cloned.1.call-update) | async-done | bytes 1048592 | tf_op jit(solution)/shard_map/all_gather | solution.py:60
  238.1 1.7 convolution_bitcast_fusion
  241.6 10.8 %reduce-scatter.11.cloned.1.call-done = f32[128,256]{1,0:T(8,128)} async-done(((f32[256,256]{1,0:T(8,128)}), f32[128,256]{1,0:T(8,128)}) %reduce-scatter.11.cloned.1.call-update) | async-done | bytes 131088 | tf_op jit(solution)/shard_map/reduce_scatter | solution.py:74
  252.4 1.6 multiply_subtract_fusion
  (63 shorter events, 19.2 us)
Async XLA Ops:
  6.5 0.7 copy-start.8
  6.5 0.7 copy-start.9
  7.2 1.0 copy-start.6
  20.4 7.6 %copy-start.4 = (f32[128,256]{1,0:T(8,128)S(1)}, f32[128,256]{1,0:T(8,128)}, u32[]{:S(2)}) copy-start(f32[128,256]{1,0:T(8,128)} %param.5) | copy-start | bytes 393220
  20.4 31.6 %all-to-all-start = ((bf16[16,2,1,1,1,128,128]{6,5,1,4,3,2,0:T(8,128)(2,1)}), bf16[16,2,1,1,1,128,128]{6,5,1,4,3,2,0:T(8,128)(2,1)S(1)}, u32[]{:S(2)}, u32[]{:S(2)}) async-start(bf16[16,2,1,1,1,128,128]{6,5,1,4,3,2,0:T(8,128)(2,1)} %fusion.12), calls=%async_computation | async-start | bytes 2097152 | tf_op jit(solution)/shard_map/all_to_all | solution.py:34
  28.0 46.8 %all-gather.5.cloned.1.call-start = ((), (), s32[]{:S(2)}) async-start(), calls=%async_computation.6 | async-start | bytes 1114112 | tf_op jit(solution)/shard_map/all_gather | solution.py:60
  53.1 18.0 %all-to-all-start.1 = ((bf16[2,1,16,1,128,128]{5,4,2,3,1,0:T(8,128)(2,1)}), bf16[2,1,16,1,128,128]{5,4,2,3,1,0:T(8,128)(2,1)S(1)}, u32[]{:S(2)}, u32[]{:S(2)}) async-start(bf16[2,1,16,1,128,128]{5,4,2,3,1,0:T(8,128)(2,1)} %copy.57), calls=%async_computation.1 | async-start | bytes 2097152 | tf_op jit(solution)/shard_map/all_to_all | solution.py:32
  56.6 32.8 %reduce-scatter.5.cloned.1.call-start = ((), (), s32[]{:S(2)}) async-start(), calls=%async_computation.7 | async-start | bytes 393216 | tf_op jit(solution)/shard_map/reduce_scatter | solution.py:74
  77.4 0.7 copy-start.1
  77.4 0.8 copy-start.7
  78.1 51.4 %all-gather.7.cloned.1.call-start = ((), (), s32[]{:S(2)}) async-start(), calls=%async_computation.8 | async-start | bytes 1114112 | tf_op jit(solution)/shard_map/all_gather | solution.py:60
  91.0 52.8 %reduce-scatter.7.cloned.1.call-start = ((), (), s32[]{:S(2)}) async-start(), calls=%async_computation.9 | async-start | bytes 393216 | tf_op jit(solution)/shard_map/reduce_scatter | solution.py:74
  132.2 0.7 copy-start.2
  132.9 50.8 %all-gather.9.cloned.1.call-start = ((), (), s32[]{:S(2)}) async-start(), calls=%async_computation.10 | async-start | bytes 1114112 | tf_op jit(solution)/shard_map/all_gather | solution.py:60
  145.4 52.6 %reduce-scatter.9.cloned.1.call-start = ((), (), s32[]{:S(2)}) async-start(), calls=%async_computation.11 | async-start | bytes 393216 | tf_op jit(solution)/shard_map/reduce_scatter | solution.py:74
  186.4 0.7 copy-start.3
  187.1 51.0 %all-gather.11.cloned.1.call-start = ((), (), s32[]{:S(2)}) async-start(), calls=%async_computation.12 | async-start | bytes 1114112 | tf_op jit(solution)/shard_map/all_gather | solution.py:60
  199.6 52.8 %reduce-scatter.11.cloned.1.call-start = ((), (), s32[]{:S(2)}) async-start(), calls=%async_computation.13 | async-start | bytes 393216 | tf_op jit(solution)/shard_map/reduce_scatter | solution.py:74
  240.8 0.7 copy-start
  240.8 11.6 %copy-start.5 = (f32[128,256]{1,0:T(8,128)S(1)}, f32[128,256]{1,0:T(8,128)}, u32[]{:S(2)}) copy-start(f32[128,256]{1,0:T(8,128)} %reduce-scatter.9.cloned.1.call-done) | copy-start | bytes 393220
Sparse Core Ops, SparseCore 0:
  30.9 43.7 all-gather.4
  78.3 11.1 reduce-scatter.4
  91.6 37.8 all-gather.6
  133.1 10.7 reduce-scatter.6
  145.8 37.8 all-gather.8
  187.3 10.7 reduce-scatter.8
  200.2 37.8 all-gather.10
  241.6 10.7 reduce-scatter.10
